TPU v7x, 256 devices: a whole 4x4x8 slice. The times are simulated.
256 devices in a mesh: loop: 4 (over x_lo, core), sub: 64 (over z, y, x_hi).
Axes of the slice: x: 4 (x_hi: 2, x_lo: 2; x = x_hi * 2 + x_lo), y: 4, z: 8, core: 2. Of those that a mesh axis runs over, the one named last changes fastest.
Arguments:
- rate: float32 [8192, 5, 384], P(('loop', 'sub')), may hold values from 0 to 1
- phase: float32 [8192, 5, 384], P(('loop', 'sub')), may hold values from -3.140625 to 3.140625
- forcing: float32 [2, 4, 8192, 5, 384], P(None, None, ('loop', 'sub')), may hold values from -8 to 8
Outputs:
- response: float32 [2, 4, 8192, 5, 384], P(None, None, ('loop', 'sub'))
All inputs are finite; a program needn't handle non-finite values.
Results may differ from a plain program's by a relative error of at most 0.0003.
Values sent between devices are 32-bit elements; how exact they have to be, the bound alone decides.
A program may use at most 128 MiB of HBM per device.

v0:
```python
import jax
import jax.numpy as jnp
from jax import lax
from jax.sharding import PartitionSpec as P

fringe_total = 0.7


def carried_in(value, axis, join, neutral):
    count, mine = (lax.axis_size(axis), lax.axis_index(axis))
    pieces = jax.tree.map(lambda part: lax.all_gather(part, axis), value)
    subtotal = jax.tree.map(
        lambda part, zero: jnp.full_like(part, 0) + jnp.asarray(zero, part.dtype), value, neutral
    )

    def hop(position, subtotal):
        longer = join(subtotal, jax.tree.map(lambda part: part[position], pieces))
        return jax.tree.map(lambda new, old: jnp.where(position < mine, new, old), longer, subtotal)

    return lax.fori_loop(0, count - 1, hop, subtotal)


def broadcast(value, axis, source):
    kept = jnp.where(lax.axis_index(axis) == source, value, 0).astype(value.dtype)
    return lax.psum(kept, axis)


def complex_product(left, right):
    return jnp.stack(
        [left[0] * right[0] - left[1] * right[1], left[0] * right[1] + left[1] * right[0]]
    )


def compose(earlier, later):
    return (complex_product(later[0], earlier[0]), complex_product(later[0], earlier[1]) + later[1])


def local(rate, phase, forcing):
    stations = rate.shape[0]
    devices = lax.axis_size(("loop", "sub"))
    is_last = lax.axis_index(("loop", "sub")) == devices - 1
    fringe_sponge = jnp.where(
        is_last, jnp.float32(fringe_total ** (1.0 / stations)), jnp.float32(1.0)
    )
    magnitude = jnp.exp(-rate) * fringe_sponge
    coeff = jnp.stack([magnitude * jnp.cos(phase), magnitude * jnp.sin(phase)])[:, None]
    source = jnp.sqrt(-jnp.expm1(-2.0 * rate)) * forcing
    local_a, local_b = lax.associative_scan(compose, (coeff, source), axis=2)
    own = (local_a[:, :, -1], local_b[:, :, -1])
    unit = (
        jnp.stack([jnp.ones_like(own[0][0]), jnp.zeros_like(own[0][0])]),
        jnp.zeros_like(own[1]),
    )
    before = carried_in((own[0], own[1]), ("loop", "sub"), compose, unit)
    through = compose(before, own)
    circuit_transfer = (
        broadcast(through[0], ("loop", "sub"), devices - 1),
        broadcast(through[1], ("loop", "sub"), devices - 1),
    )
    denom_re = 1.0 - circuit_transfer[0][0]
    denom_im = -circuit_transfer[0][1]
    scale = denom_re * denom_re + denom_im * denom_im
    closing = complex_product(circuit_transfer[1], jnp.stack([denom_re, -denom_im])) / scale
    entering = complex_product(before[0], closing) + before[1]
    return local_b + complex_product(local_a, entering[:, :, None])


def solution(mesh):
    placed = (
        P(("loop", "sub"), None, None),
        P(("loop", "sub"), None, None),
        P(None, None, ("loop", "sub"), None, None),
    )
    return jax.shard_map(
        local,
        mesh=mesh,
        in_specs=placed,
        out_specs=P(None, None, ("loop", "sub"), None, None),
        check_vma=False,
    )
```

profile of v0, /device:TPU:1, one launch (start us, length us, event | category | flops | bytes accessed | tf_op | source)
XLA Modules:
  0.0 2151.6 jit_solution(167800945347909830)
XLA Ops:
  6.5 2.1 multiply_bitcast_fusion.1
  14.3 2.9 copy_multiply_fusion
  22.9 7.1 pad.65
  31.4 14.1 pad.67
  46.3 1.1 multiply_subtract_fusion.9
  47.4 1.0 maximum_add_fusion.7
  49.2 18.9 pad.66
  68.1 2.0 add.312
  70.0 1.3 multiply_subtract_fusion.5
  72.4 28.2 %pad.68 = f32[2,4,16,5,384]{4,1,3,2,0:T(4,128)S(1)} pad(f32[2,4,8,5,384]{4,1,3,2,0:T(4,128)} %pad_maximum_fusion.1, f32[]{:T(128)} %constant.47.clone.1), padding=0_0_0x0_0_0x0_1_1x0_0_0x0_0_0 | pad | bytes 1474564 | tf_op jit(solution)/shard_map/pad | solution.py:48
  100.6 25.2 %pad.69 = f32[2,4,16,5,384]{4,1,3,2,0:T(4,128)} pad(f32[2,4,8,5,384]{4,1,3,2,0:T(4,128)S(1)} %copy-done.7, f32[]{:T(128)} %constant.47.clone.1), padding=0_0_0x0_0_0x1_0_1x0_0_0x0_0_0 | pad | bytes 1474564 | tf_op jit(solution)/shard_map/pad | solution.py:48
  125.8 2.4 add.315
  128.2 71.2 %pad.71 = f32[2,4,32,5,384]{4,1,3,2,0:T(4,128)} pad(f32[2,4,16,5,384]{4,1,3,2,0:T(4,128)} %add.315, f32[]{:T(128)} %constant.47.clone.1), padding=0_0_0x0_0_0x1_0_1x0_0_0x0_0_0 | pad | bytes 2949124 | tf_op jit(solution)/shard_map/pad | solution.py:48
  199.5 1.5 multiply_subtract_fusion.3
  202.1 49.6 %pad.70 = f32[2,4,32,5,384]{4,1,3,2,0:T(4,128)} pad(f32[2,4,16,5,384]{4,1,3,2,0:T(4,128)S(1)} %pad_maximum_fusion, f32[]{:T(128)} %constant.47.clone.1), padding=0_0_0x0_0_0x0_1_1x0_0_0x0_0_0 | pad | bytes 2949124 | tf_op jit(solution)/shard_map/pad | solution.py:48
  251.7 1.5 slice_add_fusion.8
  253.5 1.8 add_bitcast_fusion
  255.3 469.6 %all-gather.5.cloned.1.call-done = f32[512,1,1,5,384]{4,2,3,1,0:T(1,128)} async-done(((f32[2,1,1,5,384]{4,2,3,1,0:T(1,128)}), f32[512,1,1,5,384]{4,2,3,1,0:T(1,128)}) %all-gather.5.cloned.1.call-update) | async-done | bytes 3932176 | tf_op jit(solution)/shard_map/all_gather | solution.py:11
  724.9 731.3 %all-gather.7.cloned.1.call-done = f32[512,4,1,5,384]{4,1,3,2,0:T(4,128)} async-done(((f32[2,4,1,5,384]{4,1,3,2,0:T(4,128)}), f32[512,4,1,5,384]{4,1,3,2,0:T(4,128)}) %all-gather.7.cloned.1.call-update) | async-done | bytes 15728656 | tf_op jit(solution)/shard_map/all_gather | solution.py:11
  1456.2 440.8 %while.16 = (s32[]{:T(128)}, f32[2,1,5,384]{3,2,1,0:T(8,128)S(1)}, f32[2,4,5,384]{3,2,1,0:T(8,128)S(1)}, s32[]{:T(128)}, f32[256,2,1,5,384]{4,2,3,1,0:T(1,128)},...) while((s32[]{:T(128)}, f32[2,1,5,384]{3,2,1,0:T(8,128)S(1)}, ...), condition=%wide.region_1.2_spmd.clone, body=%wide.region_0.1_spmd.clone.sunk | while | flops 142085 | bytes 783507 | solution.py:20
  1897.0 0.9 fusion.14
  1899.5 1.1 copy.107
  1900.7 239.8 %all-reduce.23.cloned.1.call-done = (f32[2,4,5,384]{3,1,2,0:T(4,128)}, f32[2,1,5,384]{3,0,2,1:T(2,128)}) async-done(((f32[2,4,5,384]{3,1,2,0:T(4,128)}, f32[2,1,5,384]{3,0,2,1:T(2,128)}), (f32[2,4,5,384]{3,1,2,0:T(4,128)}, f32[2,1,5,384]{3,0,2,1:T(2,128)})) %all-reduce.23.cloned.1.call-update) | async-done | bytes 76816 | tf_op jit(solution)/shard_map/psum | solution.py:25
  2143.6 1.5 copy.117
  (2191 shorter events, 446.0 us)
Async XLA Ops:
  6.5 718.4 %all-gather.5.cloned.1.call-start = ((), (), s32[]{:S(2)}) async-start(), calls=%async_computation | async-start | bytes 3947520 | tf_op jit(solution)/shard_map/all_gather | solution.py:11
  12.3 1.8 copy-start.4
  13.3 0.8 copy-start.6
  14.0 1442.2 %all-gather.7.cloned.1.call-start = ((), (), s32[]{:S(2)}) async-start(), calls=%async_computation.1 | async-start | bytes 15790080 | tf_op jit(solution)/shard_map/all_gather | solution.py:11
  18.6 3.2 copy-start.3
  21.8 26.6 %slice-start = ((f32[2,4,8,5,384]{4,1,3,2,0:T(4,128)}), f32[2,4,1,5,384]{4,1,3,2,0:T(4,128)S(1)}, s32[]{:S(2)}) async-start(f32[2,4,8,5,384]{4,1,3,2,0:T(4,128)} %copy-done.3), calls=%async_computation.3 | async-start | bytes 122880 | tf_op jit(solution)/shard_map/slice | solution.py:48
  22.2 7.8 copy-start.8
  30.0 0.7 copy-start.9
  68.1 3.4 copy-start.14
  71.3 29.3 %copy-start.7 = (f32[2,4,8,5,384]{4,1,3,2,0:T(4,128)S(1)}, f32[2,4,8,5,384]{4,1,3,2,0:T(4,128)}, u32[]{:S(2)}) copy-start(f32[2,4,8,5,384]{4,1,3,2,0:T(4,128)} %add.312) | copy-start | bytes 1474564
  128.2 71.2 %copy-start.12 = (f32[15,5,384]{2,0,1:T(8,128)S(1)}, f32[15,5,384]{2,0,1:T(8,128)}, u32[]{:S(2)}) copy-start(f32[15,5,384]{2,0,1:T(8,128)} %get-tuple-element.213) | copy-start | bytes 345604
  128.2 71.2 %copy-start.11 = (f32[15,5,384]{2,0,1:T(8,128)S(1)}, f32[15,5,384]{2,0,1:T(8,128)}, u32[]{:S(2)}) copy-start(f32[15,5,384]{2,0,1:T(8,128)} %get-tuple-element.212) | copy-start | bytes 345604
  201.0 0.8 copy-start.13
  202.1 49.6 %copy-start = (f32[2,4,32,5,384]{4,1,3,2,0:T(4,128)S(1)}, f32[2,4,32,5,384]{4,1,3,2,0:T(4,128)}, u32[]{:S(2)}) copy-start(f32[2,4,32,5,384]{4,1,3,2,0:T(4,128)} %pad.71) | copy-start | bytes 5898244
  202.1 51.4 %copy-start.5 = (f32[2,1,32,5,384]{4,2,3,1,0:T(8,128)S(1)}, f32[2,1,32,5,384]{4,2,3,1,0:T(8,128)}, u32[]{:S(2)}) copy-start(f32[2,1,32,5,384]{4,2,3,1,0:T(8,128)} %copy-done.4) | copy-start | bytes 1474564
  202.1 1254.1 %copy-start.2 = (f32[2,1,5,384]{3,2,1,0:T(8,128)S(1)}, f32[2,1,5,384]{3,2,1,0:T(8,128)}, u32[]{:S(2)}) copy-start(f32[2,1,5,384]{3,2,1,0:T(8,128)} %constant.49.clone.1) | copy-start | bytes 46084
  253.2 1887.2 %all-reduce.23.cloned.1.call-start = ((), (), s32[]{:S(2)}) async-start(), calls=%async_computation.2 | async-start | bytes 153600 | tf_op jit(solution)/shard_map/psum | solution.py:25
  1456.2 441.8 %copy-start.10 = (f32[2,4,1,5,384]{4,1,3,2,0:T(4,128)S(1)}, f32[2,4,1,5,384]{4,1,3,2,0:T(4,128)}, u32[]{:S(2)}) copy-start(f32[2,4,1,5,384]{4,1,3,2,0:T(4,128)} %slice_add_fusion.8) | copy-start | bytes 184324
  2140.5 2.2 copy-start.1
Sparse Core Ops, SparseCore 0:
  14.1 710.7 all-gather.4
  726.8 729.3 all-gather.6
  1899.5 240.9 all-reduce.22
where the time goes:
time: 2180 us; the launch traced here: 2150 us
  waiting for transfers between devices  1440 us (66%)
  local copies, waits for them, and re-layouts  627 us (29%)
  other arithmetic  54.5 us (2%)
    all_gather x2, waiting for transfers between devices, carried_in(): pieces = jax.tree.map(lambda part: lax.all_gather(part, axis), value)  1200 us
    psum x1, waiting for transfers between devices, broadcast(): return lax.psum(kept, axis)  240 us
    pad x16, local copies, waits for them, and re-layouts, local(): local_a, local_b = lax.associative_scan(compose, (coeff, source), axis=2)  216 us
    dynamic_slice x255, local copies, waits for them, and re-layouts, hop(): longer = join(subtotal, jax.tree.map(lambda part: part[position], pieces))  215 us
    slice x255, local copies, waits for them, and re-layouts, complex_product(): left[1] * right[1]  185 us
  transfers between devices with their start and end apart: 3, of which 3 were waited for; matrix products, arithmetic and copies ran while one was open for 11% of the time, Pallas kernels for 0%

commit v1 on v0

--- a/solution.py
+++ b/solution.py
@@ -22,7 +22,7 @@
 
 def broadcast(value, axis, source):
     kept = jnp.where(lax.axis_index(axis) == source, value, 0).astype(value.dtype)
-    return lax.psum(kept, axis)
+    return jnp.sum(lax.all_gather(kept, axis), axis=0)
 
 
 def complex_product(left, right):

time: 2180 us -> 3390 us (1.56)
  waiting for transfers between devices: 1440 us -> 2640 us
    all_gather x0 -> x2, waiting for transfers between devices: none -> 1430 us  [broadcast(): return jnp.sum(lax.all_gather(kept, axis), axis=0)]
    psum x1 -> x0, waiting for transfers between devices: 240 us -> none  [broadcast(): return lax.psum(kept, axis)]
  transfers between devices with their start and end apart: 3 -> 4, of which waited for: 3 -> 4; matrix products, arithmetic and copies ran while one was open for 11% -> 7% of each run, Pallas kernels for 0% -> 0%
where the time goes in v1:
time: 3390 us; the launch traced here: 3350 us
  waiting for transfers between devices  2640 us (78%)
  local copies, waits for them, and re-layouts  627 us (18%)
  other arithmetic  61.3 us (2%)
    all_gather x2, waiting for transfers between devices, broadcast(): return jnp.sum(lax.all_gather(kept, axis), axis=0)  1430 us
    all_gather x2, waiting for transfers between devices, carried_in(): pieces = jax.tree.map(lambda part: lax.all_gather(part, axis), value)  1200 us
    pad x16, local copies, waits for them, and re-layouts, local(): local_a, local_b = lax.associative_scan(compose, (coeff, source), axis=2)  216 us
    dynamic_slice x255, local copies, waits for them, and re-layouts, hop(): longer = join(subtotal, jax.tree.map(lambda part: part[position], pieces))  215 us
    slice x255, local copies, waits for them, and re-layouts, complex_product(): left[1] * right[1]  185 us
  transfers between devices with their start and end apart: 4, of which 4 were waited for; matrix products, arithmetic and copies ran while one was open for 7% of the time, Pallas kernels for 0%

profile of v1, /device:TPU:1, one launch (start us, length us, event | category | flops | bytes accessed | tf_op | source)
XLA Modules:
  0.0 3354.5 jit_solution(15454094883601345141)
XLA Ops:
  6.5 2.1 multiply_bitcast_fusion.1
  14.2 2.9 copy_multiply_fusion
  22.8 7.1 pad.65
  31.3 14.1 pad.67
  46.2 1.1 multiply_subtract_fusion.9
  47.3 1.0 maximum_add_fusion.7
  49.1 18.9 pad.66
  68.0 1.9 add.318
  69.9 1.3 multiply_subtract_fusion.5
  72.3 28.2 pad.68
  100.5 25.2 pad.69
  125.7 2.4 add.321
  128.1 71.2 %pad.71 = f32[2,4,32,5,384]{4,1,3,2,0:T(4,128)} pad(f32[2,4,16,5,384]{4,1,3,2,0:T(4,128)} %add.321, f32[]{:T(128)} %constant.47.clone.1), padding=0_0_0x0_0_0x1_0_1x0_0_0x0_0_0 | pad | bytes 2949124 | tf_op jit(solution)/shard_map/pad | solution.py:48
  199.4 1.5 multiply_subtract_fusion.3
  202.0 49.6 %pad.70 = f32[2,4,32,5,384]{4,1,3,2,0:T(4,128)} pad(f32[2,4,16,5,384]{4,1,3,2,0:T(4,128)S(1)} %pad_maximum_fusion, f32[]{:T(128)} %constant.47.clone.1), padding=0_0_0x0_0_0x0_1_1x0_0_0x0_0_0 | pad | bytes 2949124 | tf_op jit(solution)/shard_map/pad | solution.py:48
  251.7 1.5 slice_add_fusion.8
  253.2 471.7 %all-gather.11.cloned.1.call-done = f32[512,1,1,5,384]{4,2,3,1,0:T(1,128)} async-done(((f32[2,1,1,5,384]{4,2,3,1,0:T(1,128)}), f32[512,1,1,5,384]{4,2,3,1,0:T(1,128)}) %all-gather.11.cloned.1.call-update) | async-done | bytes 3932176 | tf_op jit(solution)/shard_map/all_gather | solution.py:11
  724.9 731.3 %all-gather.13.cloned.1.call-done = f32[512,4,1,5,384]{4,1,3,2,0:T(4,128)} async-done(((f32[2,4,1,5,384]{4,1,3,2,0:T(4,128)}), f32[512,4,1,5,384]{4,1,3,2,0:T(4,128)}) %all-gather.13.cloned.1.call-update) | async-done | bytes 15728656 | tf_op jit(solution)/shard_map/all_gather | solution.py:11
  1456.2 440.9 %while.16 = (s32[]{:T(128)}, f32[2,1,5,384]{3,2,1,0:T(8,128)S(1)}, f32[2,4,5,384]{3,2,1,0:T(8,128)S(1)}, s32[]{:T(128)}, f32[256,2,1,5,384]{4,2,3,1,0:T(1,128)},...) while((s32[]{:T(128)}, f32[2,1,5,384]{3,2,1,0:T(8,128)S(1)}, ...), condition=%wide.region_1.2_spmd.clone, body=%wide.region_0.1_spmd.clone.sunk | while | flops 142085 | bytes 783507 | solution.py:20
  1899.3 705.2 %all-gather.9.cloned.1.call-done = f32[256,2,1,5,384]{4,1,3,2,0:T(2,128)} async-done(((f32[1,2,1,5,384]{4,1,3,2,0:T(2,128)}), f32[256,2,1,5,384]{4,1,3,2,0:T(2,128)}) %all-gather.9.cloned.1.call-update) | async-done | bytes 3932176 | tf_op jit(solution)/shard_map/all_gather | solution.py:25
  2604.5 3.2 reduce_sum.19
  2607.8 727.8 %all-gather.7.cloned.1.call-done = f32[256,2,4,5,384]{4,2,3,1,0:T(4,128)} async-done(((f32[1,2,4,5,384]{4,2,3,1,0:T(4,128)}), f32[256,2,4,5,384]{4,2,3,1,0:T(4,128)}) %all-gather.7.cloned.1.call-update) | async-done | bytes 15728656 | tf_op jit(solution)/shard_map/all_gather | solution.py:25
  3335.6 8.4 reduce_sum.18
  3346.5 1.5 copy.160
  (2199 shorter events, 445.7 us)
Async XLA Ops:
  6.5 718.4 %all-gather.11.cloned.1.call-start = ((), (), s32[]{:S(2)}) async-start(), calls=%async_computation.2 | async-start | bytes 3947520 | tf_op jit(solution)/shard_map/all_gather | solution.py:11
  12.2 1.8 copy-start.4
  13.3 0.8 copy-start.6
  14.0 1442.2 %all-gather.13.cloned.1.call-start = ((), (), s32[]{:S(2)}) async-start(), calls=%async_computation.3 | async-start | bytes 15790080 | tf_op jit(solution)/shard_map/all_gather | solution.py:11
  18.6 3.1 copy-start.3
  21.8 26.6 slice-start
  22.1 7.8 copy-start.9
  29.9 0.7 copy-start.10
  68.0 3.4 copy-start.15
  71.2 29.3 copy-start.8
  128.1 71.2 %copy-start.13 = (f32[15,5,384]{2,0,1:T(8,128)S(1)}, f32[15,5,384]{2,0,1:T(8,128)}, u32[]{:S(2)}) copy-start(f32[15,5,384]{2,0,1:T(8,128)} %get-tuple-element.217) | copy-start | bytes 345604
  128.1 71.2 %copy-start.12 = (f32[15,5,384]{2,0,1:T(8,128)S(1)}, f32[15,5,384]{2,0,1:T(8,128)}, u32[]{:S(2)}) copy-start(f32[15,5,384]{2,0,1:T(8,128)} %get-tuple-element.216) | copy-start | bytes 345604
  200.9 0.8 copy-start.14
  202.0 49.7 %copy-start = (f32[2,4,32,5,384]{4,1,3,2,0:T(4,128)S(1)}, f32[2,4,32,5,384]{4,1,3,2,0:T(4,128)}, u32[]{:S(2)}) copy-start(f32[2,4,32,5,384]{4,1,3,2,0:T(4,128)} %pad.71) | copy-start | bytes 5898244
  202.0 1254.2 %copy-start.2 = (f32[2,1,5,384]{3,2,1,0:T(8,128)S(1)}, f32[2,1,5,384]{3,2,1,0:T(8,128)}, u32[]{:S(2)}) copy-start(f32[2,1,5,384]{3,2,1,0:T(8,128)} %constant.49.clone.1) | copy-start | bytes 46084
  253.2 2351.3 %all-gather.9.cloned.1.call-start = ((), (), s32[]{:S(2)}) async-start(), calls=%async_computation.1 | async-start | bytes 3947520 | tf_op jit(solution)/shard_map/all_gather | solution.py:25
  1456.2 440.9 %copy-start.5 = (f32[2,1,32,5,384]{4,2,3,1,0:T(8,128)S(1)}, f32[2,1,32,5,384]{4,2,3,1,0:T(8,128)}, u32[]{:S(2)}) copy-start(f32[2,1,32,5,384]{4,2,3,1,0:T(8,128)} %copy-done.4) | copy-start | bytes 1474564
  1456.2 440.9 %copy-start.7 = (f32[2,1,32,5,384]{4,2,3,1,0:T(8,128)S(1)}, f32[2,1,32,5,384]{4,2,3,1,0:T(8,128)}, u32[]{:S(2)}) copy-start(f32[2,1,32,5,384]{4,2,3,1,0:T(8,128)} %copy-done.6) | copy-start | bytes 1474564
  1456.2 442.0 %copy-start.11 = (f32[2,4,1,5,384]{4,1,3,2,0:T(4,128)S(1)}, f32[2,4,1,5,384]{4,1,3,2,0:T(4,128)}, u32[]{:S(2)}) copy-start(f32[2,4,1,5,384]{4,1,3,2,0:T(4,128)} %slice_add_fusion.8) | copy-start | bytes 184324
  1897.9 1437.7 %all-gather.7.cloned.1.call-start = ((), (), s32[]{:S(2)}) async-start(), calls=%async_computation | async-start | bytes 15790080 | tf_op jit(solution)/shard_map/all_gather | solution.py:25
  3344.1 1.5 copy-start.1
Sparse Core Ops, SparseCore 0:
  14.1 710.7 all-gather.10
  726.8 729.3 all-gather.12
  1898.0 706.4 all-gather.8
  2606.2 729.3 all-gather.6
